TPU v7x, 256 devices: a whole 4x4x8 slice. The times are simulated.
256 devices in a mesh: wide: 64 (over z, y, core), narrow: 4 (over x).
Axes of the slice: x: 4, y: 4, z: 8, core: 2. Of those that a mesh axis runs over, the one named last changes fastest.
Arguments:
- stored_amps: float32 [1024, 16384], P('wide', 'narrow'), may hold values from -6 to 6
- integrals: float32 [16384, 16384], P('narrow', 'wide'), may hold values from -0.046875 to 0.046875
- pair_counts: int32 [4], replicated, may hold values from 2048 to 4096, as said below
- block_map: int32 [64], replicated, may hold values from 0 to 63, each once
Outputs:
- cycle_out: float32 [1024, 16384], P('wide', 'narrow')
Inputs may be any that keep to these rules, and one draw needn't show every extreme that they name: `pair_counts`: each count lies between half of 4096 and 4096; one count equals 4096. `block_map`: a permutation of the indices of wide.
All inputs are finite; a program needn't handle non-finite values.
Results may differ from a plain program's by a relative error of at most 0.000086.
Values sent between devices are 32-bit elements; how exact they have to be, the bound alone decides.
No kernel may reach another device: no remote copies, remote signals or barrier semaphores. Data moves between devices by JAX's collectives and lax.ppermute only.
A program may use at most 64 MiB of HBM per device.

v0:
```python
import jax
import jax.numpy as jnp
from jax import lax
from jax.sharding import PartitionSpec as P

PB = 4096
BR = 8


def true_order(rows_block, block_map, count_wide):
    total = rows_block.shape[0]
    width = rows_block.shape[1]
    slots = total // (count_wide * BR)
    shaped = rows_block.reshape(count_wide, slots, BR, width)
    shaped = jnp.take(shaped, block_map, axis=0)
    return jnp.transpose(shaped, (1, 0, 2, 3)).reshape(total, width)


def on_device(stored_amps, integrals, pair_counts, block_map):
    count_wide = lax.axis_size("wide")
    count_narrow = lax.axis_size("narrow")
    layer = lax.axis_index("narrow")
    width = stored_amps.shape[1]
    columns = layer * width + jnp.arange(width, dtype=jnp.int32)
    owner = columns // PB
    limit = jnp.sum(
        jnp.where(
            owner[:, None] == jnp.arange(4, dtype=jnp.int32)[None, :], pair_counts[None, :], 0
        ),
        axis=1,
    )
    masked = jnp.where((columns % PB < limit)[None, :], stored_amps, jnp.float32(0.0))
    local_cols = integrals.shape[1]
    cycle = jnp.dot(
        lax.all_gather(masked, "wide", axis=0, tiled=True),
        integrals,
        precision=lax.Precision.HIGHEST,
        preferred_element_type=jnp.float32,
    )
    ordered = true_order(cycle, block_map, count_wide)
    moved = lax.all_to_all(ordered, "wide", split_axis=0, concat_axis=1, tiled=True)
    height = moved.shape[0]
    group = local_cols // count_narrow
    moved = moved.reshape(height, count_wide, count_narrow, group)
    moved = jnp.transpose(moved, (0, 2, 1, 3)).reshape(height, count_wide * local_cols)
    cycle_out = lax.psum_scatter(moved, "narrow", scatter_dimension=1, tiled=True)
    return cycle_out


def solution(mesh):
    placed = (P("wide", "narrow"), P("narrow", "wide"), P(), P())
    return jax.shard_map(
        on_device, mesh=mesh, in_specs=placed, out_specs=P("wide", "narrow"), check_vma=False
    )
```

profile of v0, /device:TPU:8, one launch (start us, length us, event | category | flops | bytes accessed | tf_op | source)
XLA Modules:
  0.0 200.3 jit_solution(17723670310562345288)
XLA Ops:
  6.5 0.0 all-gather.2.cloned.1.call-start
  6.6 0.8 select_reduce_fusion
  7.4 1.7 broadcast_select_fusion
  9.0 0.0 all-gather.2.cloned.1.call-update
  9.1 0.0 reduce-scatter.2.cloned.1.call-start
  9.1 0.7 compare_select_fusion
  9.8 0.7 compare_and_fusion
  10.4 100.6 %all-gather.2.cloned.1.call-done = f32[1024,4096]{1,0:T(8,128)} async-done(((f32[16,4096]{1,0:T(8,128)}), f32[1024,4096]{1,0:T(8,128)}) %all-gather.2.cloned.1.call-update) | async-done | bytes 16777232 | tf_op jit(solution)/shard_map/all_gather | solution.py:35
  111.0 16.2 %fusion.6 = f32[1024,256]{1,0:T(8,128)S(1)} fusion(f32[1024,4096]{1,0:T(8,128)} %all-gather.2.cloned.1.call-done, f32[4096,256]{1,0:T(8,128)} %param.5), kind=kOutput, calls=%fused_computation.21 | convolution fusion | flops 12884901888 | bytes 22020096 | tf_op jit(solution)/shard_map/dot_general | solution.py:34
  127.2 0.6 gather_fusion
  127.9 0.1 select_bitcast_fusion
  128.0 0.1 copy.9
  128.1 36.1 %all_to_all.16 = f32[64,16,256]{2,1,0:T(8,128)S(1)} all-to-all(f32[64,16,256]{2,1,0:T(8,128)S(1)} %bitcast.11), channel_id=1, replica_groups=mesh['wide'=64,'narrow'=4] {'wide'}, dimensions={0} | all-to-all | bytes 2097152 | tf_op jit(solution)/shard_map/all_to_all | solution.py:41
  164.2 0.6 copy.10
  164.8 0.9 reshape.59
  165.7 1.7 copy.11
  167.4 3.2 %reshape.60 = f32[16,16384]{1,0:T(8,128)} reshape(f32[16,4,64,64]{3,2,1,0:T(8,128)} %copy.11) | data formatting | bytes 2097152 | tf_op jit(solution)/shard_map/reshape | solution.py:45
  170.6 0.0 reduce-scatter.2.cloned.1.call-update
  170.6 22.9 %reduce-scatter.2.cloned.1.call-done = f32[16,4096]{1,0:T(8,128)} async-done(((f32[16,16384]{1,0:T(8,128)}), f32[16,4096]{1,0:T(8,128)}) %reduce-scatter.2.cloned.1.call-update) | async-done | bytes 262160 | tf_op jit(solution)/shard_map/reduce_scatter | solution.py:46
  (3 shorter events, 0.0 us)
Async XLA Ops:
  6.5 104.5 %all-gather.2.cloned.1.call-start = ((), (), s32[]{:S(2)}) async-start(), calls=%async_computation.2 | async-start | bytes 17039360 | tf_op jit(solution)/shard_map/all_gather | solution.py:35
  9.1 184.4 %reduce-scatter.2.cloned.1.call-start = ((), (), s32[]{:S(2)}) async-start(), calls=%async_computation.3 | async-start | bytes 1310720 | tf_op jit(solution)/shard_map/reduce_scatter | solution.py:46
Sparse Core Ops, SparseCore 0:
  10.1 100.8 all-gather.1
  170.7 22.6 reduce-scatter.1
where the time goes:
time: 201 us; the launch traced here: 200 us
  waiting for transfers between devices  123 us (61%)
  blocking collectives  36.1 us (18%)
  matrix products  16.2 us (8%)
  between operations  13.5 us (7%)
  local copies, waits for them, and re-layouts  7.09 us (4%)
  other arithmetic  3.96 us (2%)
    all_gather x1, waiting for transfers between devices, on_device(): lax.all_gather(masked, 'wide', axis=0, tiled=True)  101 us
    all_to_all x1, blocking collectives, on_device(): lax.all_to_all(ordered, 'wide', split_axis=0, concat_axis=1, tiled=True)  36.1 us
    reduce_scatter x1, waiting for transfers between devices, on_device(): lax.psum_scatter(moved, 'narrow', scatter_dimension=1, tiled=True)  22.9 us
    dot_general x1, matrix products, on_device(): jnp.dot(lax.all_gather(masked, 'wide', axis=0, tiled=True), integrals, pr...  16.2 us
  transfers between devices with their start and end apart: 2, of which 2 were waited for; matrix products, arithmetic and copies ran while one was open for 1% of the time, Pallas kernels for 0%

commit v1 on v0

--- a/solution.py
+++ b/solution.py
@@ -5,6 +5,15 @@
 
 PB = 4096
 BR = 8
+
+
+def supply_all_the_units(slab_in):
+    return jnp.concatenate(
+        lax.all_to_all(
+            jnp.stack([slab_in for _ in range(lax.axis_size("wide"))], axis=0), "wide", 0, 0
+        ),
+        0,
+    )
 
 
 def true_order(rows_block, block_map, count_wide):
@@ -32,7 +41,7 @@
     masked = jnp.where((columns % PB < limit)[None, :], stored_amps, jnp.float32(0.0))
     local_cols = integrals.shape[1]
     cycle = jnp.dot(
-        lax.all_gather(masked, "wide", axis=0, tiled=True),
+        supply_all_the_units(masked),
         integrals,
         precision=lax.Precision.HIGHEST,
         preferred_element_type=jnp.float32,

time: 201 us -> 491 us (2.44)
  waiting for transfers between devices: 123 us -> 392 us
  starting transfers between devices: 0.04 us -> 12.5 us
  local copies, waits for them, and re-layouts: 7.09 us -> 14.9 us
    all_to_all x0 -> x1, waiting for transfers between devices: none -> 369 us  [supply_all_the_units(): lax.all_to_all(jnp.stack([slab_in for _ in range(lax.axis_size('wide'))],...]
    all_gather x1 -> x0, waiting for transfers between devices: 101 us -> none  [on_device(): lax.all_gather(masked, 'wide', axis=0, tiled=True)]
    all_to_all x0 -> x1, starting transfers between devices: none -> 12.4 us  [supply_all_the_units(): lax.all_to_all(jnp.stack([slab_in for _ in range(lax.axis_size('wide'))],...]
    another operation x0 -> x1, local copies, waits for them, and re-layouts: none -> 7.8 us  [supply_all_the_units(): jnp.stack([slab_in for _ in range(lax.axis_size('wide'))], axis=0)]
  transfers between devices with their start and end apart: 2 -> 2, of which waited for: 2 -> 2; matrix products, arithmetic and copies ran while one was open for 1% -> 0% of each run, Pallas kernels for 0% -> 0%
where the time goes in v1:
time: 491 us
  waiting for transfers between devices  392 us (80%)
  blocking collectives  40.1 us (8%)
  matrix products  16.2 us (3%)
  local copies, waits for them, and re-layouts  14.9 us (3%)
  between operations  13.5 us (3%)
  starting transfers between devices  12.5 us (3%)
    all_to_all x1, waiting for transfers between devices, supply_all_the_units(): lax.all_to_all(jnp.stack([slab_in for _ in range(lax.axis_size('wide'))],...  369 us
    all_to_all x1, blocking collectives, on_device(): lax.all_to_all(ordered, 'wide', split_axis=0, concat_axis=1, tiled=True)  40.1 us
    reduce_scatter x1, waiting for transfers between devices, on_device(): lax.psum_scatter(moved, 'narrow', scatter_dimension=1, tiled=True)  22.8 us
    dot_general x1, matrix products, on_device(): jnp.dot(supply_all_the_units(masked), integrals, precision=lax.Precision....  16.2 us
    all_to_all x1, starting transfers between devices, supply_all_the_units(): lax.all_to_all(jnp.stack([slab_in for _ in range(lax.axis_size('wide'))],...  12.4 us
  transfers between devices with their start and end apart: 2, of which 2 were waited for; matrix products, arithmetic and copies ran while one was open for 0% of the time, Pallas kernels for 0%

profile of v1, /device:TPU:8, one launch (start us, length us, event | category | flops | bytes accessed | tf_op | source)
XLA Modules:
  0.0 490.6 jit_solution(4500557127652575807)
XLA Ops:
  6.6 0.8 select_reduce_fusion
  7.3 1.0 broadcast_select_fusion
  8.3 7.8 %stack.2 = f32[64,16,4096]{2,1,0:T(8,128)} broadcast(f32[16,4096]{1,0:T(8,128)S(1)} %broadcast_select_fusion), dimensions={1,2} | broadcast | bytes 17039360 | tf_op jit(solution)/shard_map/stack | solution.py:13
  16.1 0.0 copy-start
  16.1 12.4 %all-to-all-start = ((f32[64,16,4096]{2,1,0:T(8,128)}), f32[64,16,4096]{2,1,0:T(8,128)}, u32[]{:S(2)}, u32[]{:S(2)}) async-start(f32[64,16,4096]{2,1,0:T(8,128)} %stack.2), calls=%async_computation | async-start | bytes 33554432 | tf_op jit(solution)/shard_map/all_to_all | solution.py:12
  28.6 0.0 reduce-scatter.2.cloned.1.call-start
  28.6 0.0 copy-done
  28.7 368.7 %all-to-all-done = f32[64,16,4096]{2,1,0:T(8,128)} async-done(((f32[64,16,4096]{2,1,0:T(8,128)}), f32[64,16,4096]{2,1,0:T(8,128)}, u32[]{:S(2)}, u32[]{:S(2)}) %all-to-all-start) | async-done | bytes 16777248 | tf_op jit(solution)/shard_map/all_to_all | solution.py:12
  397.4 16.2 %fusion = f32[64,2,8,256]{3,2,1,0:T(8,128)S(1)} fusion(f32[64,16,4096]{2,1,0:T(8,128)} %all-to-all-done, f32[4096,256]{1,0:T(8,128)} %param.5), kind=kOutput, calls=%fused_computation.1 | convolution fusion | flops 12884901888 | bytes 22020096 | tf_op jit(solution)/shard_map/dot_general | solution.py:43
  413.6 0.6 gather_fusion
  414.2 0.1 select_bitcast_fusion
  414.4 0.1 copy.10
  414.5 40.1 %all_to_all.21 = f32[64,16,256]{2,1,0:T(8,128)S(1)} all-to-all(f32[64,16,256]{2,1,0:T(8,128)S(1)} %bitcast.16), channel_id=1, replica_groups=mesh['wide'=64,'narrow'=4] {'wide'}, dimensions={0} | all-to-all | bytes 2097152 | tf_op jit(solution)/shard_map/all_to_all | solution.py:50
  454.5 0.6 copy.11
  455.1 0.9 reshape.61
  456.0 1.7 copy.12
  457.7 3.2 reshape.62
  460.9 0.0 reduce-scatter.2.cloned.1.call-update
  460.9 22.8 %reduce-scatter.2.cloned.1.call-done = f32[16,4096]{1,0:T(8,128)} async-done(((f32[16,16384]{1,0:T(8,128)}), f32[16,4096]{1,0:T(8,128)}) %reduce-scatter.2.cloned.1.call-update) | async-done | bytes 262160 | tf_op jit(solution)/shard_map/reduce_scatter | solution.py:55
  (5 shorter events, 0.1 us)
Async XLA Ops:
  16.1 12.5 %copy-start = (s32[64]{0:T(128)S(1)}, s32[64]{0:T(128)}, u32[]{:S(2)}) copy-start(s32[64]{0:T(128)} %param.7) | copy-start | bytes 772
  16.1 381.2 %all-to-all-start = ((f32[64,16,4096]{2,1,0:T(8,128)}), f32[64,16,4096]{2,1,0:T(8,128)}, u32[]{:S(2)}, u32[]{:S(2)}) async-start(f32[64,16,4096]{2,1,0:T(8,128)} %stack.2), calls=%async_computation | async-start | bytes 33554432 | tf_op jit(solution)/shard_map/all_to_all | solution.py:12
  28.6 455.2 %reduce-scatter.2.cloned.1.call-start = ((), (), s32[]{:S(2)}) async-start(), calls=%async_computation.3 | async-start | bytes 1310720 | tf_op jit(solution)/shard_map/reduce_scatter | solution.py:55
Sparse Core Ops, SparseCore 0:
  461.1 22.6 reduce-scatter.1
